TPU v7x, 512 devices: a whole 4x4x16 slice. The times are simulated.
512 devices in a mesh: row: 16 (over y_lo, x, core), col: 32 (over z, y_hi).
Axes of the slice: x: 4, y: 4 (y_hi: 2, y_lo: 2; y = y_hi * 2 + y_lo), z: 16, core: 2. Of those that a mesh axis runs over, the one named last changes fastest.
Arguments:
- activations: bfloat16 [512, 28672], P('row', 'col'), may hold values from -160 to 160
- down_weight: bfloat16 [28672, 256], P(('row', 'col')), may hold values from -6 to 6
- keep_mask: int32 [28672, 256], P(('row', 'col')), may hold values 0 or 1
Outputs:
- gram_damped: bfloat16 [28672, 28672], P('row', 'col')
- updated: bfloat16 [28672, 256], P(('row', 'col'))
All inputs are finite; a program needn't handle non-finite values. No bound on the sum of `keep_mask` on one device may be relied on, other than what follows from the above.
Results may differ from a plain program's by a relative error of at most 0.017.
Values may be sent and summed in bfloat16 or wider, within the bound.
A program may use at most 64 MiB of HBM per device.

v0:
```python
import functools

import jax
import jax.numpy as jnp
from jax import lax
from jax.sharding import Mesh
from jax.sharding import PartitionSpec as P

FF = 28672
ROWS = 512
ROW = ("row_0", "row_1", "row_2")
COL = ("col_0", "col_1")
ROW_COL = ("row_0", "row_1", "row_2", "col_0", "col_1")


damp_ratio = 0.1
step_ratio = 0.25


def by_axis(x, axes):
    return functools.reduce(lax.psum, axes, x)


def joined_along(pieces, dim):
    pieces = jnp.moveaxis(pieces, 0, dim)
    dims = pieces.shape
    return pieces.reshape(*dims[:dim], dims[dim] * dims[dim + 1], *dims[dim + 2 :])


def from_everyone(x, axis):
    copies = jnp.broadcast_to(x, (lax.axis_size(axis), *x.shape))
    return lax.all_to_all(copies, axis, split_axis=0, concat_axis=0, tiled=True)


def gathered_copies(x, axis, dim):
    return joined_along(from_everyone(x, axis), dim)


def from_root(x, axes, root):
    x = jnp.where(lax.axis_index(axes) == root, x, jnp.zeros_like(x))
    for axis in axes:
        x = lax.psum(x, axis)
    return x


def whole_of(x, axes, dim):
    if not axes:
        return x
    nearer = lax.all_gather(x, axes[-1], axis=dim, tiled=True)
    return whole_of(nearer, axes[:-1], dim)


def from_root_2(x, axis, root):
    return lax.dynamic_index_in_dim(lax.all_gather(x, axis), root, 0, keepdims=False)


def over_copies(x, axis):
    everything = from_everyone(x, axis)
    return jnp.sum(everything.astype(jnp.float32), axis=0)


def local(activations, down_weight, keep_mask):
    row_count = lax.axis_size(ROW)
    col_count = lax.axis_size(COL)
    panel_ratio = col_count // row_count
    row_index = lax.axis_index(ROW)
    col_index = lax.axis_index(COL)
    panel_width = activations.shape[1]
    own_rows = down_weight.shape[0]
    act_float = activations.astype(jnp.float32)
    square_sum = by_axis(jnp.sum(act_float * act_float), ROW_COL)
    mean_square = square_sum / (ROWS * FF) + 1e-06
    damping = damp_ratio * mean_square
    col_panel = gathered_copies(activations, ROW, 0)
    halves = []
    tile_parts = []
    for part_index in range(panel_ratio):
        half_panel = from_root(col_panel, COL, row_index * panel_ratio + part_index)
        halves.append(half_panel)
        tile_parts.append(
            lax.dot_general(
                half_panel, col_panel, (((0,), (0,)), ((), ())), preferred_element_type=jnp.float32
            )
            / ROWS
        )
    gram_tile = jnp.concatenate(tile_parts, axis=0)
    tile_rows = gram_tile.shape[0]
    global_rows = row_index * tile_rows + lax.iota(jnp.int32, tile_rows)
    global_cols = col_index * panel_width + lax.iota(jnp.int32, panel_width)
    gram_damped = (
        gram_tile
        + jnp.where(global_rows[:, None] == global_cols[None, :], damping, jnp.float32(0.0))
    ).astype(jnp.bfloat16)
    pruned = down_weight * (1 - keep_mask).astype(jnp.bfloat16)
    pruned_panel = whole_of(pruned, COL, 0)
    offset = col_index % panel_ratio * panel_width
    local_slab = lax.dynamic_slice_in_dim(pruned_panel, offset, panel_width, 0)
    pruned_block = from_root_2(local_slab, ROW, col_index // panel_ratio)
    partial_value = jnp.dot(activations, pruned_block, preferred_element_type=jnp.float32)
    sample_block = over_copies(partial_value.astype(jnp.bfloat16), COL).astype(jnp.float32)
    samples = gathered_copies(sample_block.astype(jnp.bfloat16), ROW, 0).astype(sample_block.dtype)
    which_half = col_index // row_count
    inner = col_index % row_count * own_rows
    picked = jnp.zeros((ROWS, own_rows), jnp.bfloat16)
    for part_index in range(panel_ratio):
        columns = lax.dynamic_slice_in_dim(halves[part_index], inner, own_rows, 1)
        picked = jnp.where(which_half == part_index, columns, picked)
    descent = (
        lax.dot_general(
            picked.astype(jnp.float32),
            samples,
            (((0,), (0,)), ((), ())),
            precision=lax.Precision.HIGHEST,
        )
        / ROWS
    )
    keep_float = keep_mask.astype(jnp.float32)
    updated = keep_float * (
        down_weight.astype(jnp.float32) + step_ratio * descent / ((1.0 + damp_ratio) * mean_square)
    )
    return (gram_damped, updated.astype(jnp.bfloat16))


def solution(mesh):
    torus = Mesh(
        mesh.devices.reshape(2, 4, 2, 16, 2), ("row_0", "row_1", "row_2", "col_0", "col_1")
    )
    in_specs = (P(ROW, COL), P(ROW_COL, None), P(ROW_COL, None))
    out_specs = (P(ROW, COL), P(ROW_COL, None))
    return jax.shard_map(local, mesh=torus, in_specs=in_specs, out_specs=out_specs, check_vma=False)
```

profile of v0, /device:TPU:7, one launch (start us, length us, event | category | flops | bytes accessed | tf_op | source)
XLA Modules:
  0.0 288.4 jit_solution(16914826326774945970)
XLA Ops:
  8.0 1.8 broadcast_in_dim.22
  9.8 9.7 %all-to-all-start = ((bf16[16,32,896]{2,1,0:T(8,128)(2,1)}), bf16[16,32,896]{2,1,0:T(8,128)(2,1)S(1)}, u32[]{:S(2)}, u32[]{:S(2)}) async-start(bf16[16,32,896]{2,1,0:T(8,128)(2,1)} %broadcast_in_dim.22), calls=%async_computation | async-start | bytes 1835008 | tf_op jit(solution)/shard_map/all_to_all | solution.py:32
  19.6 12.4 %all-to-all-done = bf16[16,32,896]{2,1,0:T(8,128)(2,1)S(1)} async-done(((bf16[16,32,896]{2,1,0:T(8,128)(2,1)}), bf16[16,32,896]{2,1,0:T(8,128)(2,1)S(1)}, u32[]{:S(2)}, u32[]{:S(2)}) %all-to-all-start) | async-done | bytes 917536 | tf_op jit(solution)/shard_map/all_to_all | solution.py:32
  31.9 1.6 broadcast_select_fusion.1
  33.7 5.2 %all_gather.12 = bf16[112,256]{1,0:T(8,128)(2,1)S(1)} all-gather(bf16[56,256]{1,0:T(8,128)(2,1)S(1)} %fusion.15), channel_id=1, replica_groups=mesh['row_0'=2,'row_1'=4,'row_2'=2,'col_0'=16,'col_1'=2] {'col_1'}, dimensions={0}, use_global_device_ids=true | all-gather | bytes 86016 | tf_op jit(solution)/shard_map/all_gather | solution.py:49
  38.9 33.7 %all_gather.13 = bf16[1792,256]{1,0:T(8,128)(2,1)S(1)} all-gather(bf16[112,256]{1,0:T(8,128)(2,1)S(1)} %all_gather.12), channel_id=1, replica_groups=mesh['row_0'=2,'row_1'=4,'row_2'=2,'col_0'=16,'col_1'=2] {'col_0'}, dimensions={0}, use_global_device_ids=true | all-gather | bytes 974848 | tf_op jit(solution)/shard_map/all_gather | solution.py:49
  72.6 0.8 constant_dynamic-slice_fusion
  73.4 95.5 %all-reduce.5.cloned.1.call-done = (bf16[512,896]{1,0:T(8,128)(2,1)}, bf16[512,896]{1,0:T(8,128)(2,1)}) async-done(((bf16[512,896]{1,0:T(8,128)(2,1)}, bf16[512,896]{1,0:T(8,128)(2,1)}), (bf16[512,896]{1,0:T(8,128)(2,1)}, bf16[512,896]{1,0:T(8,128)(2,1)})) %all-reduce.5.cloned.1.call-update) | async-done | bytes 1835024 | tf_op jit(solution)/shard_map/psum | solution.py:42
  169.0 1.2 fusion.5
  170.2 0.9 broadcast_in_dim.26
  171.1 9.3 %all-to-all-start.1 = ((bf16[32,32,256]{2,1,0:T(8,128)(2,1)}), bf16[32,32,256]{2,1,0:T(8,128)(2,1)}, u32[]{:S(2)}, u32[]{:S(2)}) async-start(bf16[32,32,256]{2,1,0:T(8,128)(2,1)} %broadcast_in_dim.26), calls=%async_computation.1 | async-start | bytes 1048576 | tf_op jit(solution)/shard_map/all_to_all | solution.py:32
  181.0 4.4 %psum.67 = f32[]{:T(128)} all-reduce(f32[]{:T(128)} %multiply_reduce_fusion), channel_id=1, replica_groups=mesh['row_0'=2,'row_1'=4,'row_2'=2,'col_0'=16,'col_1'=2] {'row_0'}, use_global_device_ids=true, to_apply=%region_5.0 | all-reduce | flops 1 | bytes 8 | tf_op jit(solution)/shard_map/psum | solution.py:21
  185.4 6.4 %psum.68 = f32[]{:T(128)} all-reduce(f32[]{:T(128)} %psum.67), channel_id=1, replica_groups=mesh['row_0'=2,'row_1'=4,'row_2'=2,'col_0'=16,'col_1'=2] {'row_1'}, use_global_device_ids=true, to_apply=%region_6.7 | all-reduce | flops 1 | bytes 8 | tf_op jit(solution)/shard_map/psum | solution.py:21
  191.7 16.9 %psum.69 = f32[]{:T(128)} all-reduce(f32[]{:T(128)} %psum.68), channel_id=1, replica_groups=mesh['row_0'=2,'row_1'=4,'row_2'=2,'col_0'=16,'col_1'=2] {'row_2'}, use_global_device_ids=true, to_apply=%region_7.8 | all-reduce | flops 1 | bytes 8 | tf_op jit(solution)/shard_map/psum | solution.py:21
  208.6 25.2 %psum.70 = f32[]{:T(128)} all-reduce(f32[]{:T(128)} %psum.69), channel_id=1, replica_groups=mesh['row_0'=2,'row_1'=4,'row_2'=2,'col_0'=16,'col_1'=2] {'col_0'}, use_global_device_ids=true, to_apply=%region_8.9 | all-reduce | flops 1 | bytes 8 | tf_op jit(solution)/shard_map/psum | solution.py:21
  233.8 5.9 %psum.71 = f32[]{:T(128)} all-reduce(f32[]{:T(128)} %psum.70), channel_id=1, replica_groups=mesh['row_0'=2,'row_1'=4,'row_2'=2,'col_0'=16,'col_1'=2] {'col_1'}, use_global_device_ids=true, to_apply=%region_9.10 | all-reduce | flops 1 | bytes 8 | tf_op jit(solution)/shard_map/psum | solution.py:21
  240.4 20.0 %all-reduce.7.cloned.1.call-done = (bf16[512,896]{1,0:T(8,128)(2,1)}, bf16[512,896]{1,0:T(8,128)(2,1)}) async-done(((bf16[512,896]{1,0:T(8,128)(2,1)}, bf16[512,896]{1,0:T(8,128)(2,1)}), (bf16[512,896]{1,0:T(8,128)(2,1)}, bf16[512,896]{1,0:T(8,128)(2,1)})) %all-reduce.7.cloned.1.call-update) | async-done | bytes 1835024 | tf_op jit(solution)/shard_map/psum | solution.py:42
  260.4 2.7 convolution_multiply_fusion
  263.1 2.8 convolution_multiply_fusion.1
  266.0 1.1 reduce_sum.22
  267.8 5.3 %all-to-all-start.2 = ((bf16[16,32,256]{2,1,0:T(8,128)(2,1)}), bf16[16,32,256]{2,1,0:T(8,128)(2,1)S(1)}, u32[]{:S(2)}, u32[]{:S(2)}) async-start(bf16[16,32,256]{2,1,0:T(8,128)(2,1)} %broadcast_in_dim.27), calls=%async_computation.2 | async-start | bytes 524288 | tf_op jit(solution)/shard_map/all_to_all | solution.py:32
  273.1 4.4 %fusion = bf16[1792,896]{1,0:T(8,128)(2,1)} fusion(f32[896,896]{1,0:T(8,128)S(1)} %convolution_multiply_fusion, f32[896,896]{1,0:T(8,128)} %convolution_multiply_fusion.1, f32[]{:T(128)S(6)} %mul_shard_map.6, s32[896]{0:T(1024)S(1)} %iota_add_fusion.1, s32[1792]{0:T(1024)S(1)} %iota_add_fusion), kind=kLoop, calls=%fused_computation.1 | loop fusion | flops 8028160 | bytes 9644548 | tf_op jit(solution)/shard_map/convert_element_type | solution.py:93
  277.5 1.5 all-to-all-done.2
  279.0 2.0 fusion.4
  (25 shorter events, 1.6 us)
Async XLA Ops:
  9.8 23.8 %copy-start.4 = (s32[56,256]{1,0:T(8,128)S(1)}, s32[56,256]{1,0:T(8,128)}, u32[]{:S(2)}) copy-start(s32[56,256]{1,0:T(8,128)} %param.5) | copy-start | bytes 172036
  9.8 23.8 %copy-start.5 = (bf16[56,256]{1,0:T(8,128)(2,1)S(1)}, bf16[56,256]{1,0:T(8,128)(2,1)}, u32[]{:S(2)}) copy-start(bf16[56,256]{1,0:T(8,128)(2,1)} %param.4) | copy-start | bytes 86020
  9.8 22.1 %all-to-all-start = ((bf16[16,32,896]{2,1,0:T(8,128)(2,1)}), bf16[16,32,896]{2,1,0:T(8,128)(2,1)S(1)}, u32[]{:S(2)}, u32[]{:S(2)}) async-start(bf16[16,32,896]{2,1,0:T(8,128)(2,1)} %broadcast_in_dim.22), calls=%async_computation | async-start | bytes 1835008 | tf_op jit(solution)/shard_map/all_to_all | solution.py:32
  19.5 149.4 %all-reduce.5.cloned.1.call-start = ((), (), s32[]{:S(2)}) async-start(), calls=%async_computation.4 | async-start | bytes 3670016 | tf_op jit(solution)/shard_map/psum | solution.py:42
  31.9 41.4 %copy-start = (bf16[16,32,896]{2,1,0:T(8,128)(2,1)}, bf16[16,32,896]{2,1,0:T(8,128)(2,1)S(1)}, u32[]{:S(2)}) copy-start(bf16[16,32,896]{2,1,0:T(8,128)(2,1)S(1)} %all-to-all-done) | copy-start | bytes 2752516
  33.5 135.5 %copy-start.3 = (bf16[32,896]{1,0:T(8,128)(2,1)S(1)}, bf16[32,896]{1,0:T(8,128)(2,1)}, u32[]{:S(2)}) copy-start(bf16[32,896]{1,0:T(8,128)(2,1)} %param.3) | copy-start | bytes 172036
  33.6 135.4 %all-gather.3.cloned.1.call-start = ((), (), s32[]{:S(2)}) async-start(), calls=%async_computation.3 | async-start | bytes 7798784 | tf_op jit(solution)/shard_map/all_gather | solution.py:54
  73.4 187.0 %all-reduce.7.cloned.1.call-start = ((), (), s32[]{:S(2)}) async-start(), calls=%async_computation.5 | async-start | bytes 3670016 | tf_op jit(solution)/shard_map/psum | solution.py:42
  171.1 94.9 %all-to-all-start.1 = ((bf16[32,32,256]{2,1,0:T(8,128)(2,1)}), bf16[32,32,256]{2,1,0:T(8,128)(2,1)}, u32[]{:S(2)}, u32[]{:S(2)}) async-start(bf16[32,32,256]{2,1,0:T(8,128)(2,1)} %broadcast_in_dim.26), calls=%async_computation.1 | async-start | bytes 1048576 | tf_op jit(solution)/shard_map/all_to_all | solution.py:32
  260.4 2.7 copy-start.1
  260.4 2.8 copy-start.2
  267.8 11.2 %all-to-all-start.2 = ((bf16[16,32,256]{2,1,0:T(8,128)(2,1)}), bf16[16,32,256]{2,1,0:T(8,128)(2,1)S(1)}, u32[]{:S(2)}, u32[]{:S(2)}) async-start(bf16[16,32,256]{2,1,0:T(8,128)(2,1)} %broadcast_in_dim.27), calls=%async_computation.2 | async-start | bytes 524288 | tf_op jit(solution)/shard_map/all_to_all | solution.py:32
Sparse Core Ops, SparseCore 0:
  33.7 135.2 all-reduce.4
  171.9 88.4 all-reduce.6
Sparse Core Ops, SparseCore 1:
  73.5 58.3 all-gather.2
where the time goes:
time: 291 us; the launch traced here: 288 us
  waiting for transfers between devices  129 us (44%)
  blocking collectives  97.6 us (34%)
  starting transfers between devices  24.4 us (8%)
  between operations  16.3 us (6%)
  matrix products  8.73 us (3%)
  other arithmetic  7.77 us (3%)
  local copies, waits for them, and re-layouts  4.21 us (1%)
    psum x2, waiting for transfers between devices, from_root(): x = lax.psum(x, axis)  115 us
    psum x5, blocking collectives, by_axis(): return functools.reduce(lax.psum, axes, x)  58.7 us
    all_gather x2, blocking collectives, whole_of(): nearer = lax.all_gather(x, axes[-1], axis=dim, tiled=True)  38.9 us
    all_to_all x3, starting transfers between devices, from_everyone(): return lax.all_to_all(copies, axis, split_axis=0, concat_axis=0, tiled=True)  24.2 us
    all_to_all x3, waiting for transfers between devices, from_everyone(): return lax.all_to_all(copies, axis, split_axis=0, concat_axis=0, tiled=True)  13.8 us
  transfers between devices with their start and end apart: 6, of which 4 were waited for; matrix products, arithmetic and copies ran while one was open for 5% of the time, Pallas kernels for 0%

commit v1 on v0

v1 whole, which is shorter than its diff:
```python
import functools

import jax
import jax.numpy as jnp
from jax import lax
from jax.experimental import pallas as pl
from jax.experimental.pallas import tpu as pltpu
from jax.sharding import Mesh
from jax.sharding import PartitionSpec as P

MESH = pl.DeviceIdType.MESH
AXES = ("row_0", "row_1", "row_2", "col_0", "col_1")
ROW = AXES[:3]
COL = AXES[3:]
F32 = jnp.float32
BF16 = jnp.bfloat16
SUB = 2

damp_ratio = 0.1
step_ratio = 0.25


def exchange_kernel(
    nx,
    nz,
    a_ref,
    dw_ref,
    mask_ref,
    rowp_ref,
    colp_ref,
    s_ref,
    q_ref,
    zbuf,
    pown,
    pbuf,
    pfull,
    spart,
    yx_send,
    yx_recv,
    yq_send,
    yq_recv,
    zs_buf,
    zq_buf,
    ring_send,
    ring_recv,
    row_send,
    row_recv,
    col_send,
    col_recv,
    perm_sem,
    pag_send,
    pag_recv,
    yx_sem,
    zs_send,
    zs_recv,
    zq_send,
    zq_recv,
    pln_send,
    pln_recv,
):
    nr = 4 * nx
    own = dw_ref.shape[0]
    rows, width = a_ref.shape
    half = rows // 2
    sub_rows = rows // SUB
    yl, x, k, z, yh = (lax.axis_index(name) for name in AXES)
    r = (yl * nx + x) * 2 + k
    chip = yl * nx + x
    plane = 2 * r + yh

    def dev(r_, z_, yh_):
        return dict(
            row_0=lax.div(r_, 2 * nx),
            row_1=lax.rem(lax.div(r_, 2), nx),
            row_2=lax.rem(r_, 2),
            col_0=z_,
            col_1=yh_,
        )

    def remote(src, dst, send, recv, to):
        return pltpu.make_async_remote_copy(
            src_ref=src, dst_ref=dst, send_sem=send, recv_sem=recv, device_id=to, device_id_type=MESH
        )

    t_r, t_z, t_yh = 2 * lax.rem(z, nz // 2) + yh, r, lax.div(z, nz // 2)
    s_r, s_z, s_yh = z, yh * (nz // 2) + lax.div(r, 2), lax.rem(r, 2)
    fixed = (t_r == r) & (t_z == z) & (t_yh == yh)

    barrier = pltpu.get_barrier_semaphore()

    def greet(to):
        pl.semaphore_signal(barrier, inc=1, device_id=to, device_id_type=MESH)

    greet(dev(t_r, t_z, t_yh))
    greet(dev(s_r, s_z, s_yh))
    for off in range(1, nz):
        greet(dev(r, lax.rem(z + off, nz), yh))
    for off in range(1, 2 * nr):
        other = lax.rem(plane + off, 2 * nr)
        greet(dev(lax.div(other, 2), z, lax.rem(other, 2)))

    pown[0:own, :] = dw_ref[...] * (1 - mask_ref[...]).astype(BF16)
    act = a_ref[...].astype(F32)
    square = jnp.sum(jnp.sum(act * act, axis=0, keepdims=True), axis=1, keepdims=True)
    square = jnp.broadcast_to(square, (8, 256))
    high = square.astype(BF16).astype(F32)
    middle = (square - high).astype(BF16).astype(F32)
    low = (square - high - middle).astype(BF16).astype(F32)
    line = lax.broadcasted_iota(jnp.int32, (8, 256), 0)
    zero = jnp.zeros((8, 256), F32)
    coded = jnp.where(line == 0, high, jnp.where(line == 1, middle, jnp.where(line == 2, low, zero)))
    pown[own : own + 8, :] = coded.astype(BF16)

    pl.semaphore_wait(barrier, 2 + (nz - 1) + (2 * nr - 1))

    perm = remote(pown, pbuf.at[r], perm_sem.at[0], perm_sem.at[1], dev(t_r, t_z, t_yh))
    perm_out = remote(pown, pbuf.at[t_r], perm_sem.at[0], perm_sem.at[1], dev(t_r, t_z, t_yh))
    perm_here = pltpu.make_async_copy(pown, pbuf.at[r], perm_sem.at[1])

    @pl.when(jnp.logical_not(fixed))
    def _():
        perm_out.start()

    @pl.when(fixed)
    def _():
        perm_here.start()

    plus, minus = lax.rem(z + 1, nz), lax.rem(z + nz - 1, nz)
    hops = (nz // 2, nz - 1 - nz // 2)

    def ring_block(way, step):
        return lax.rem(z - step + nz, nz) if way == 0 else lax.rem(z + step, nz)

    def piece(block, step, sub):
        if step == 0:
            return a_ref.at[pl.ds(sub * sub_rows, sub_rows)]
        return zbuf.at[block, sub]

    def ring_copy(way, step, sub):
        block = ring_block(way, step)
        to = plus if way == 0 else minus
        return remote(
            piece(block, step, sub),
            zbuf.at[block, sub],
            ring_send.at[way, step, sub],
            ring_recv.at[way, step, sub],
            dev(r, to, yh),
        )

    def row_copy(block, step, to_yh, sub):
        return remote(
            piece(block, step, sub),
            rowp_ref.at[yh, r, sub],
            row_send.at[block, to_yh, sub],
            row_recv.at[yh, r, sub],
            dev(block, z, to_yh),
        )

    def row_local(block, step, sub):
        return pltpu.make_async_copy(piece(block, step, sub), rowp_ref.at[yh, r, sub], row_recv.at[yh, r, sub])

    def row_start(block, step, sub):
        for to_yh in range(2):
            here = (block == r) & (yh == to_yh)

            @pl.when(jnp.logical_not(here))
            def _():
                row_copy(block, step, to_yh, sub).start()

            @pl.when(here)
            def _():
                row_local(block, step, sub).start()

    def col_copy(off):
        other = lax.rem(chip + off, 2 * nx)
        return remote(a_ref, colp_ref.at[r], col_send.at[off], col_recv.at[r], dev(2 * other + k, z, yh))

    def col_from(off):
        return 2 * lax.rem(chip - off + 2 * nx, 2 * nx) + k

    def col_wait(source):
        remote(a_ref, colp_ref.at[source], col_send.at[0], col_recv.at[source], dev(r, z, yh)).wait_recv()

    def col_pass(off):
        source = col_from(off)
        src = a_ref if off == 0 else colp_ref.at[source]
        return remote(src, colp_ref.at[source], col_send.at[2 * nx + off], col_recv.at[source], dev(2 * chip + 1 - k, z, yh))

    col_own = pltpu.make_async_copy(a_ref, colp_ref.at[r], col_recv.at[r])

    for sub in range(SUB):
        for way in range(2):
            ring_copy(way, 0, sub).start()
    for sub in range(SUB):
        row_start(z, 0, sub)
    for off in range(1, 2 * nx):
        col_copy(off).start()
    col_pass(0).start()
    col_own.start()

    def ring_step(step):
        for sub in range(SUB):
            for way in range(2):
                if step < hops[way]:
                    ring_copy(way, step, sub).wait_recv()
                    block = ring_block(way, step + 1)
                    if step + 1 < hops[way]:
                        ring_copy(way, step + 1, sub).start()
                    row_start(block, step + 1, sub)

    def pag_copy(off):
        other = lax.rem(chip + off, 2 * nx)
        return remote(pbuf.at[r], pbuf.at[r], pag_send.at[off], pag_recv.at[r], dev(2 * other + k, z, yh))

    def pag_wait(source):
        remote(pown, pbuf.at[source], pag_send.at[0], pag_recv.at[source], dev(r, z, yh)).wait_recv()

    def pag_pass(off):
        source = col_from(off)
        return remote(
            pbuf.at[source], pbuf.at[source], pag_send.at[2 * nx + off], pag_recv.at[source], dev(2 * chip + 1 - k, z, yh)
        )

    def sum_start():
        perm.wait_recv()
        for off in range(1, 2 * nx):
            pag_copy(off).start()
        pag_pass(0).start()

    def sum_pass():
        for off in range(1, 2 * nx):
            pag_wait(col_from(off))
            pag_pass(off).start()

    yx_copy = remote(yx_send, yx_recv, yx_sem.at[0], yx_sem.at[1], dev(r, z, 1 - yh))
    yq_copy = remote(yq_send, yq_recv, yx_sem.at[2], yx_sem.at[3], dev(r, z, 1 - yh))

    def sum_partial():
        for off in range(2 * nx):
            pag_wait(2 * lax.rem(chip + off, 2 * nx) + 1 - k)
        total = jnp.zeros((8, 128), F32)
        for source in range(nr):
            held = pbuf[source, 0:own, :].astype(F32)
            pfull[source * own : (source + 1) * own, :] = held
            total = total + pbuf[source, own : own + 8, 0:128].astype(F32)
        yq_send[...] = jnp.sum(total, axis=0, keepdims=True)
        spart[...] = jnp.dot(a_ref[...], pfull[...].astype(BF16), preferred_element_type=F32)
        yx_send[...] = spart[pl.ds(pl.multiple_of((1 - yh) * half, 8), half), :].astype(BF16)
        yx_copy.start()
        yq_copy.start()

    def zs_copy(off):
        to = dev(r, lax.rem(z + off, nz), yh)
        return remote(zs_buf.at[z], zs_buf.at[z], zs_send.at[off], zs_recv.at[z], to)

    def zq_copy(off):
        to = dev(r, lax.rem(z + off, nz), yh)
        return remote(zq_buf.at[z], zq_buf.at[z], zq_send.at[off], zq_recv.at[z], to)

    def sum_across():
        yx_copy.wait_recv()
        yq_copy.wait_recv()
        both = spart[pl.ds(pl.multiple_of(yh * half, 8), half), :] + yx_recv[...].astype(F32)
        zs_buf[z] = both.astype(BF16)
        zq_buf[z] = yq_send[...] + yq_recv[...]
        for off in range(1, nz):
            zs_copy(off).start()
        for off in range(1, nz):
            zq_copy(off).start()

    def pln_copy(off):
        other = lax.rem(plane + off, 2 * nr)
        to = dev(lax.div(other, 2), z, lax.rem(other, 2))
        return remote(s_ref.at[plane], s_ref.at[plane], pln_send.at[off], pln_recv.at[plane], to)

    def sum_total():
        for off in range(1, nz):
            source = lax.rem(z + off, nz)
            remote(zs_buf.at[z], zs_buf.at[source], zs_send.at[0], zs_recv.at[source], dev(r, z, yh)).wait_recv()
            remote(zq_buf.at[z], zq_buf.at[source], zq_send.at[0], zq_recv.at[source], dev(r, z, yh)).wait_recv()
        total = zs_buf[0].astype(F32)
        squares = zq_buf[0]
        for source in range(1, nz):
            total = total + zs_buf[source].astype(F32)
            squares = squares + zq_buf[source]
        s_ref[plane] = total.astype(BF16)
        q_ref[...] = squares
        for off in range(1, 2 * nr):
            pln_copy(off).start()

    after = {2: (sum_start,), 3: (sum_pass, sum_partial), 4: (sum_across,), 6: (sum_total,)}
    last = hops[0] - 1
    for step in range(hops[0]):
        ring_step(step)
        for work in after.get(step, ()) if last == 7 else ():
            work()
    if last != 7:
        for work in (sum_start, sum_pass, sum_partial, sum_across, sum_total):
            work()

    for off in range(1, 2 * nx):
        source = col_from(off)
        col_wait(source)
        col_pass(off).start()
    for off in range(2 * nx):
        col_wait(2 * lax.rem(chip + off, 2 * nx) + 1 - k)
    col_own.wait()
    for source in range(1, 2 * nr):
        other = lax.rem(plane + source, 2 * nr)
        remote(s_ref.at[plane], s_ref.at[other], pln_send.at[0], pln_recv.at[other], dev(r, z, yh)).wait_recv()
    for from_yh in range(2):
        for source in range(nr):
            for sub in range(SUB):
                pltpu.make_async_copy(
                    piece(z, 0, sub), rowp_ref.at[from_yh, source, sub], row_recv.at[from_yh, source, sub]
                ).wait()

    @pl.when(jnp.logical_not(fixed))
    def _():
        perm_out.wait_send()

    for way in range(2):
        for step in range(hops[way]):
            for sub in range(SUB):
                ring_copy(way, step, sub).wait_send()
    for block in range(nr):
        for to_yh in range(2):

            @pl.when(jnp.logical_not((r == block) & (yh == to_yh)))
            def _():
                for sub in range(SUB):
                    row_copy(block, 0, to_yh, sub).wait_send()

    for off in range(1, 2 * nx):
        col_copy(off).wait_send()
        pag_copy(off).wait_send()
    for off in range(2 * nx):
        col_pass(off).wait_send()
        pag_pass(off).wait_send()
    yx_copy.wait_send()
    yq_copy.wait_send()
    for off in range(1, nz):
        zs_copy(off).wait_send()
        zq_copy(off).wait_send()
    for off in range(1, 2 * nr):
        pln_copy(off).wait_send()


def exchange(activations, down_weight, keep_mask):
    nx = lax.axis_size("row_1")
    nz = lax.axis_size("col_0")
    nr = 4 * nx
    rows, width = activations.shape
    own, out = down_weight.shape
    half = rows // 2
    hops = nz // 2
    dma = pltpu.SemaphoreType.DMA
    vmem = pl.BlockSpec(memory_space=pltpu.VMEM)
    hbm = pl.BlockSpec(memory_space=pl.ANY)
    return pl.pallas_call(
        functools.partial(exchange_kernel, nx, nz),
        out_shape=(
            jax.ShapeDtypeStruct((2, nr, SUB, rows // SUB, width), BF16),
            jax.ShapeDtypeStruct((nr, rows, width), BF16),
            jax.ShapeDtypeStruct((2 * nr, half, out), BF16),
            jax.ShapeDtypeStruct((1, 128), F32),
        ),
        in_specs=[vmem] * 3,
        out_specs=(hbm, hbm, vmem, vmem),
        scratch_shapes=[
            pltpu.VMEM((nz, SUB, rows // SUB, width), BF16),
            pltpu.VMEM((own + 8, out), BF16),
            pltpu.VMEM((nr, own + 8, out), BF16),
            pltpu.VMEM((width, out), F32),
            pltpu.VMEM((rows, out), F32),
            pltpu.VMEM((half, out), BF16),
            pltpu.VMEM((half, out), BF16),
            pltpu.VMEM((1, 128), F32),
            pltpu.VMEM((1, 128), F32),
            pltpu.VMEM((nz, half, out), BF16),
            pltpu.VMEM((nz, 1, 128), F32),
            dma((2, hops, SUB)),
            dma((2, hops, SUB)),
            dma((nr, 2, SUB)),
            dma((2, nr, SUB)),
            dma((4 * nx,)),
            dma((nr,)),
            dma((2,)),
            dma((4 * nx,)),
            dma((nr,)),
            dma((4,)),
            dma((nz,)),
            dma((nz,)),
            dma((nz,)),
            dma((nz,)),
            dma((2 * nr,)),
            dma((2 * nr,)),
        ],
        compiler_params=pltpu.CompilerParams(collective_id=0, has_side_effects=True),
        name="exchange",
    )(activations, down_weight, keep_mask)


def local(activations, down_weight, keep_mask):
    row_count = lax.axis_size(ROW)
    col_count = lax.axis_size(COL)
    row_index = lax.axis_index(ROW)
    col_index = lax.axis_index(COL)
    width = activations.shape[1]
    samples = activations.shape[0] * row_count
    own_rows, out = down_weight.shape
    row_panels, col_panel, s, squares = exchange(activations, down_weight, keep_mask)
    row_panels = row_panels.reshape(2, samples, width)
    col_panel = col_panel.reshape(samples, width)
    s = s.reshape(samples, out)
    mean_square = squares[0, 0] / (samples * width * col_count) + 1e-06
    damping = damp_ratio * mean_square
    tiles = []
    for part in range(2):
        tile = lax.dot_general(row_panels[part], col_panel, (((0,), (0,)), ((), ())), preferred_element_type=F32)
        tiles.append(tile / samples)
    gram_tile = jnp.concatenate(tiles, axis=0)
    tile_rows = 2 * width
    global_rows = row_index * tile_rows + lax.iota(jnp.int32, tile_rows)
    global_cols = col_index * width + lax.iota(jnp.int32, width)
    gram_damped = (
        gram_tile + jnp.where(global_rows[:, None] == global_cols[None, :], damping, jnp.float32(0.0))
    ).astype(BF16)
    picked = lax.dynamic_slice(
        row_panels, (col_index // row_count, 0, col_index % row_count * own_rows), (1, samples, own_rows)
    )[0]
    descent = lax.dot_general(picked, s, (((0,), (0,)), ((), ())), preferred_element_type=F32) / samples
    keep_float = keep_mask.astype(F32)
    updated = keep_float * (
        down_weight.astype(F32) + step_ratio * descent / ((1.0 + damp_ratio) * mean_square)
    )
    return gram_damped, updated.astype(BF16)


def solution(mesh):
    torus = Mesh(mesh.devices.reshape(2, 4, 2, 16, 2), AXES)
    in_specs = (P(ROW, COL), P(AXES, None), P(AXES, None))
    out_specs = (P(ROW, COL), P(AXES, None))
    return jax.shard_map(local, mesh=torus, in_specs=in_specs, out_specs=out_specs, check_vma=False)
```

time: 291 us -> 92.9 us (0.32)
  the two profiles are of different devices: /device:TPU:7 before, /device:TPU:24 now
where the time goes in v1:
time: 92.9 us; the launch traced here: 92.7 us
  Pallas kernels  82.2 us (88%)
  matrix products  4.24 us (5%)
  other arithmetic  3.11 us (3%)
  local copies, waits for them, and re-layouts  1.61 us (2%)
  between operations  1.5 us (2%)
    pallas_call x1, Pallas kernels, exchange(): pl.pallas_call(functools.partial(exchange_kernel, nx, nz), out_shape=(jax...  82.2 us
    convert_element_type x1, other arithmetic, local(): gram_damped = (gram_tile + jnp.where(global_rows[:, None] == global_cols[...  3.1 us
    dot_general x2, matrix products, local(): lax.dot_general(row_panels[part], col_panel, (((0,), (0,)), ((), ())), pr...  2.29 us
    dot_general x1, matrix products, local(): lax.dot_general(picked, s, (((0,), (0,)), ((), ())), preferred_element_ty...  1.95 us

profile of v1, /device:TPU:24, one launch (start us, length us, event | category | flops | bytes accessed | tf_op | source)
XLA Modules:
  0.0 92.7 jit_solution(1686064837046849094)
XLA Ops:
  0.7 82.2 %exchange.1 = (bf16[2,16,2,16,896]{4,3,2,1,0:T(8,128)(2,1)}, bf16[16,32,896]{2,1,0:T(8,128)(2,1)}, bf16[32,16,256]{2,1,0:T(8,128)(2,1)}, f32[1,128]{1,0:T(1,128)}) custom-call(bf16[32,896]{1,0:T(8,128)(2,1)} %a_ref.1, bf16[56,256]{1,0:T(8,128)(2,1)} %dw_ref.1, s32[56,256]{1,0:T(8,128)} %mask_ref.1), custom_call_target="tpu_custom_call" | custom-call | tf_op jit(solution)/shard_map/exchange/pallas_call | solution.py:360
  82.9 0.0 copy-start
  83.7 1.9 %fusion.4 = bf16[56,256]{1,0:T(8,128)(2,1)} fusion(bf16[512,256]{1,0:T(8,128)(2,1)} %bitcast.21, bf16[2,512,896]{2,1,0:T(8,128)(2,1)} %bitcast.20, s32[]{:T(128)S(6)} %select_n.23, s32[]{:T(128)S(6)} %select_n.25, bf16[56,256]{1,0:T(8,128)(2,1)} %dw_ref.1, s32[56,256]{1,0:T(8,128)} %mask_ref.1, f32[]{:T(128)} %bitcast.7), kind=kOutput, calls=%fused_computation.8 | convolution fusion | flops 14780416 | bytes 508424 | tf_op jit(solution)/shard_map/dot_general | solution.py:432
  85.7 1.6 %fusion.8 = (bf16[1,16,2,16,896]{4,3,2,1,0:T(8,128)(2,1)S(1)}, bf16[1,16,2,16,896]{4,3,2,1,0:T(8,128)(2,1)S(1)}) fusion(bf16[2,16,2,16,896]{4,3,2,1,0:T(8,128)(2,1)} %get-tuple-element.6), kind=kLoop, calls=%fused_computation.14 | loop fusion | bytes 3670016 | tf_op jit(solution)/shard_map/slice | solution.py:420
  87.3 0.0 copy-done
  87.3 1.1 %convolution_multiply_fusion = f32[896,896]{1,0:T(8,128)S(1)} fusion(bf16[512,896]{1,0:T(8,128)(2,1)S(1)} %bitcast.17, bf16[512,896]{1,0:T(8,128)(2,1)S(1)} %bitcast.18), kind=kOutput, calls=%fused_computation.2 | convolution fusion | flops 822886400 | bytes 5046272 | tf_op jit(solution)/shard_map/dot_general | solution.py:420
  88.4 1.1 %convolution_multiply_fusion.1 = f32[896,896]{1,0:T(8,128)S(1)} fusion(bf16[512,896]{1,0:T(8,128)(2,1)S(1)} %bitcast.16, bf16[512,896]{1,0:T(8,128)(2,1)S(1)} %bitcast.19), kind=kOutput, calls=%fused_computation.3 | convolution fusion | flops 822886400 | bytes 5046272 | tf_op jit(solution)/shard_map/dot_general | solution.py:420
  89.6 3.1 %fusion = bf16[1792,896]{1,0:T(8,128)(2,1)} fusion(f32[896,896]{1,0:T(8,128)S(1)} %convolution_multiply_fusion, f32[896,896]{1,0:T(8,128)S(1)} %convolution_multiply_fusion.1, f32[]{:T(128)} %bitcast.3, s32[896]{0:T(1024)S(1)} %iota_add_fusion.1, s32[1792]{0:T(1024)S(1)} %iota_add_fusion), kind=kLoop, calls=%fused_computation.1 | loop fusion | flops 8028160 | bytes 9644548 | tf_op jit(solution)/shard_map/convert_element_type | solution.py:428
  (2 shorter events, 0.0 us)
Async XLA Ops:
  82.9 4.3 %copy-start = (bf16[16,32,896]{2,1,0:T(8,128)(2,1)S(1)}, bf16[16,32,896]{2,1,0:T(8,128)(2,1)}, u32[]{:S(2)}) copy-start(bf16[16,32,896]{2,1,0:T(8,128)(2,1)} %get-tuple-element.7) | copy-start | bytes 2752516

commit v2 on v1

v2 whole, which is shorter than its diff:
```python
import functools

import jax
import jax.numpy as jnp
from jax import lax
from jax.experimental import pallas as pl
from jax.experimental.pallas import tpu as pltpu
from jax.sharding import Mesh
from jax.sharding import PartitionSpec as P

MESH = pl.DeviceIdType.MESH
AXES = ("row_0", "row_1", "row_2", "col_0", "col_1")
ROW = AXES[:3]
COL = AXES[3:]
F32 = jnp.float32
BF16 = jnp.bfloat16
SUB = 2
NEAR = 4
AFTER = {1: ("weights",), 2: ("partial",), 3: ("columns", "near")}

damp_ratio = 0.1
step_ratio = 0.25


def each(low, high, work):
    def step(i, carry):
        work(i)
        return carry

    lax.fori_loop(low, high, step, 0)


def exchange_kernel(
    nx,
    nz,
    a_ref,
    dw_ref,
    mask_ref,
    rowp_ref,
    colp_ref,
    s_ref,
    q_ref,
    zbuf,
    xbuf,
    abuf,
    pown,
    pbuf,
    pfull,
    spart,
    near_out,
    near_in,
    nearq_out,
    nearq_in,
    far_buf,
    farq_buf,
    ring_send,
    ring_recv,
    x_send,
    x_recv,
    row_send,
    row_recv,
    col_send,
    col_recv,
    perm_sem,
    pair_sem,
    pag_send,
    pag_recv,
    near_send,
    near_recv,
    nearq_send,
    nearq_recv,
    far_send,
    far_recv,
    farq_send,
    farq_recv,
    pln_send,
    pln_recv,
):
    nr = 4 * nx
    chips = 2 * nx
    own = dw_ref.shape[0]
    rows, width = a_ref.shape
    half = rows // 2
    sub_rows = rows // SUB
    yl, x, k, z, yh = (lax.axis_index(name) for name in AXES)
    chip = yl * nx + x
    r = chip * 2 + k
    plane = 2 * r + yh
    ngroup = 4 * NEAR
    nfar = nz // NEAR
    zl, zb = lax.rem(z, NEAR), lax.div(z, NEAR)
    mate = (k * NEAR + zl) * 2 + yh

    def dev(r_, z_, yh_):
        return dict(
            row_0=lax.div(r_, 2 * nx),
            row_1=lax.rem(lax.div(r_, 2), nx),
            row_2=lax.rem(r_, 2),
            col_0=z_,
            col_1=yh_,
        )

    def in_plane(flat):
        return dev(lax.div(flat, 2), z, lax.rem(flat, 2))

    def in_near(flat):
        return dev(2 * chip + lax.div(flat, 2 * NEAR), zb * NEAR + lax.rem(lax.div(flat, 2), NEAR), lax.rem(flat, 2))

    def remote(src, dst, send, recv, to):
        return pltpu.make_async_remote_copy(
            src_ref=src, dst_ref=dst, send_sem=send, recv_sem=recv, device_id=to, device_id_type=MESH
        )

    def arrived(dst, sem):
        pltpu.make_async_copy(dst, dst, sem).wait()

    t_r, t_yh = 2 * lax.rem(z, nz // 2) + yh, lax.div(z, nz // 2)
    target = dev(t_r, r, t_yh)
    source = dev(z, yh * (nz // 2) + lax.div(r, 2), lax.rem(r, 2))
    fixed = (t_r == r) & (r == z) & (t_yh == yh)

    barrier = pltpu.get_barrier_semaphore()

    def greet(to):
        pl.semaphore_signal(barrier, inc=1, device_id=to, device_id_type=MESH)

    greet(target)
    greet(source)
    greeted = 2
    each(1, nfar, lambda off: greet(dev(r, lax.rem(z + off * NEAR, nz), yh)))
    greeted += nfar - 1
    for off in (1, 2, nz - 2, nz - 1):
        greet(dev(r, lax.rem(z + off, nz), yh))
        greeted += 1
    for core in range(2):
        for to_yh in range(2):
            each(1, NEAR, lambda off: greet(dev(2 * chip + core, zb * NEAR + lax.rem(zl + off, NEAR), to_yh)))
            greeted += NEAR - 1
    each(1, 2 * nr, lambda off: greet(in_plane(lax.rem(plane + off, 2 * nr))))
    greeted += 2 * nr - 1

    pown[0:own, :] = dw_ref[...] * (1 - mask_ref[...]).astype(BF16)
    act = a_ref[...].astype(F32)
    square = jnp.sum(jnp.sum(act * act, axis=0, keepdims=True), axis=1, keepdims=True)
    square = jnp.broadcast_to(square, (8, 256))
    high = square.astype(BF16).astype(F32)
    middle = (square - high).astype(BF16).astype(F32)
    low = (square - high - middle).astype(BF16).astype(F32)
    line = lax.broadcasted_iota(jnp.int32, (8, 256), 0)
    zero = jnp.zeros((8, 256), F32)
    coded = jnp.where(line == 0, high, jnp.where(line == 1, middle, jnp.where(line == 2, low, zero)))
    pown[own : own + 8, :] = coded.astype(BF16)
    pfull[...] = jnp.zeros(pfull.shape, F32)

    pl.semaphore_wait(barrier, greeted)

    perm = remote(pown, pbuf.at[t_r], perm_sem.at[0], perm_sem.at[1], target)
    perm_here = pltpu.make_async_copy(pown, pbuf.at[r], perm_sem.at[1])

    @pl.when(jnp.logical_not(fixed))
    def _():
        perm.start()

    @pl.when(fixed)
    def _():
        perm_here.start()

    reach = (nz // 2, nz - 1 - nz // 2)

    def block_at(way, dist):
        return lax.rem(z + nz - dist, nz) if way == 0 else lax.rem(z + dist, nz)

    def piece(block, dist, sub):
        if dist == 0:
            return a_ref.at[pl.ds(pl.multiple_of(sub * sub_rows, sub_rows), sub_rows)]
        return zbuf.at[block, sub]

    def ring_copy(way, dist, sub):
        hop = 1 if dist % 2 else 2
        block = block_at(way, dist - hop)
        to = lax.rem(z + hop, nz) if way == 0 else lax.rem(z + nz - hop, nz)
        return remote(
            piece(block, dist - hop, sub),
            zbuf.at[block, sub],
            ring_send.at[way, dist - 1, sub],
            ring_recv.at[way, dist - 1, sub],
            dev(r, to, yh),
        )

    def ring_from(way, dist, sub):
        for further in (dist + 2, dist + 1):
            if further <= reach[way]:
                ring_copy(way, further, sub).start()

    def column(block):
        return lax.rem(lax.div(block, 2), nx)

    def place(block):
        return lax.div(block, 2 * nx) * 2 + lax.rem(block, 2)

    def row_copy(block, xs, sub, src, to_yh):
        rs = (yl * nx + xs) * 2 + k
        return remote(
            src,
            rowp_ref.at[yh, rs, sub],
            row_send.at[place(block), xs, to_yh, sub],
            row_recv.at[yh, rs, sub],
            dev(block, z, to_yh),
        )

    def deliver(block, xs, sub, src):
        def one(to_yh):
            here = (block == r) & (yh == to_yh)

            @pl.when(jnp.logical_not(here))
            def _():
                row_copy(block, xs, sub, src, to_yh).start()

            @pl.when(here)
            def _():
                rs = (yl * nx + xs) * 2 + k
                pltpu.make_async_copy(src, rowp_ref.at[yh, rs, sub], row_recv.at[yh, rs, sub]).start()

        each(0, 2, one)

    def x_copy(block, dist, sub):
        return remote(
            piece(block, dist, sub),
            xbuf.at[place(block), x, sub],
            x_send.at[block, sub],
            x_recv.at[place(block), x, sub],
            dev((yl * nx + column(block)) * 2 + k, z, yh),
        )

    def spread(block, dist, sub):
        @pl.when(column(block) == x)
        def _():
            deliver(block, x, sub, piece(block, dist, sub))

        @pl.when(column(block) != x)
        def _():
            x_copy(block, dist, sub).start()

    def relay(block, sub):
        @pl.when(column(block) == x)
        def _():
            def one(off):
                xs = lax.rem(x + off, nx)
                held = xbuf.at[place(block), xs, sub]
                arrived(held, x_recv.at[place(block), xs, sub])
                deliver(block, xs, sub, held)

            each(1, nx, one)

    def col_copy(off):
        other = lax.rem(chip + off, chips)
        return remote(a_ref, colp_ref.at[r], col_send.at[off], col_recv.at[r], dev(2 * other + k, z, yh))

    def col_from(off):
        return 2 * lax.rem(chip + chips - off, chips) + k

    pair = dev(2 * chip + 1 - k, z, yh)

    def col_pass(off, src):
        rs = col_from(off)
        return remote(src, colp_ref.at[rs], col_send.at[chips + off], col_recv.at[rs], pair)

    col_own = pltpu.make_async_copy(a_ref, colp_ref.at[r], col_recv.at[r])
    pair_copy = remote(a_ref, abuf, pair_sem.at[0], pair_sem.at[1], pair)

    for sub in range(SUB):
        for way in range(2):
            ring_from(way, 0, sub)
    for sub in range(SUB):
        spread(z, 0, sub)
    pair_copy.start()
    each(1, chips, lambda off: col_copy(off).start())
    col_pass(0, a_ref).start()
    col_own.start()

    def ring_round(t):
        near, far = 2 * t + 1, 2 * t + 2
        for dist in (far, near):

            def one(sub):
                for way in range(2):
                    if dist <= reach[way]:
                        block = block_at(way, dist)
                        arrived(zbuf.at[block, sub], ring_recv.at[way, dist - 1, sub])
                        if dist == far:
                            ring_from(way, dist, sub)
                        spread(block, dist, sub)

            each(0, SUB, one)

    def relay_round(t):
        for dist in (2 * t, 2 * t - 1) if t else (0,):

            def one(sub):
                for way in range(2 if t else 1):
                    if dist <= reach[way]:
                        relay(block_at(way, dist), sub)

            each(0, SUB, one)

    def pag_copy(off):
        other = lax.rem(chip + off, chips)
        return remote(pbuf.at[r], pbuf.at[r], pag_send.at[off], pag_recv.at[r], dev(2 * other + k, z, yh))

    def weights():
        arrived(pbuf.at[r], perm_sem.at[1])
        each(1, chips, lambda off: pag_copy(off).start())

    def near_copy(off):
        to = lax.rem(mate + off, ngroup)
        src = near_out.at[lax.div(to, 2 * NEAR), lax.rem(to, 2)]
        return remote(src, near_in.at[mate], near_send.at[off], near_recv.at[mate], in_near(to))

    def nearq_copy(off):
        to = in_near(lax.rem(mate + off, ngroup))
        return remote(nearq_out, nearq_in.at[mate], nearq_send.at[off], nearq_recv.at[mate], to)

    def partial():
        total = pbuf[r, own : own + 8, 0:128].astype(F32)
        pfull[pl.ds(pl.multiple_of(r * own, 8), own), :] = pbuf[r, 0:own, :].astype(F32)
        for off in range(1, chips):
            rs = col_from(off)
            arrived(pbuf.at[rs], pag_recv.at[rs])
            pfull[pl.ds(pl.multiple_of(rs * own, 8), own), :] = pbuf[rs, 0:own, :].astype(F32)
            total = total + pbuf[rs, own : own + 8, 0:128].astype(F32)
        arrived(abuf, pair_sem.at[1])
        weight = pfull[...].astype(BF16)
        mine = jnp.dot(a_ref[...], weight, preferred_element_type=F32)
        other = jnp.dot(abuf[...], weight, preferred_element_type=F32)
        spart[...] = mine
        for to_yh in range(2):
            near_out[k, to_yh] = mine[to_yh * half : (to_yh + 1) * half].astype(BF16)
            near_out[1 - k, to_yh] = other[to_yh * half : (to_yh + 1) * half].astype(BF16)
        nearq_out[...] = jnp.sum(total, axis=0, keepdims=True)
        each(1, ngroup, lambda off: near_copy(off).start())
        each(1, ngroup, lambda off: nearq_copy(off).start())

    def far_copy(off):
        to = dev(r, lax.rem(z + off * NEAR, nz), yh)
        return remote(far_buf.at[zb], far_buf.at[zb], far_send.at[off], far_recv.at[zb], to)

    def farq_copy(off):
        to = dev(r, lax.rem(z + off * NEAR, nz), yh)
        return remote(farq_buf.at[zb], farq_buf.at[zb], farq_send.at[off], farq_recv.at[zb], to)

    def near():
        total = spart[pl.ds(pl.multiple_of(yh * half, 8), half), :]
        squares = nearq_out[...]
        for off in range(1, ngroup):
            other = lax.rem(mate + off, ngroup)
            arrived(near_in.at[other], near_recv.at[other])
            total = total + near_in[other].astype(F32)
        for off in range(1, ngroup):
            other = lax.rem(mate + off, ngroup)
            arrived(nearq_in.at[other], nearq_recv.at[other])
            squares = squares + nearq_in[other]
        far_buf[zb] = total.astype(BF16)
        farq_buf[zb] = squares
        for off in range(1, nfar):
            far_copy(off).start()
            farq_copy(off).start()

    def pln_copy(off):
        to = in_plane(lax.rem(plane + off, 2 * nr))
        return remote(s_ref.at[plane], s_ref.at[plane], pln_send.at[off], pln_recv.at[plane], to)

    def far():
        for off in range(1, nfar):
            other = lax.rem(zb + off, nfar)
            arrived(far_buf.at[other], far_recv.at[other])
            arrived(farq_buf.at[other], farq_recv.at[other])
        total = far_buf[0].astype(F32)
        squares = farq_buf[0]
        for other in range(1, nfar):
            total = total + far_buf[other].astype(F32)
            squares = squares + farq_buf[other]
        s_ref[plane] = total.astype(BF16)
        q_ref[...] = squares
        each(1, 2 * nr, lambda off: pln_copy(off).start())

    def columns():
        def one(off):
            rs = col_from(off)
            arrived(colp_ref.at[rs], col_recv.at[rs])
            col_pass(off, colp_ref.at[rs]).start()

        each(1, chips, one)

    stages = dict(weights=weights, partial=partial, near=near, far=far, columns=columns)
    done = []
    rounds = (reach[0] + 1) // 2
    for t in range(rounds):
        ring_round(t)
        relay_round(t)
        for name in AFTER.get(t, ()):
            stages[name]()
            done.append(name)
    relay_round(rounds)
    for name in ("weights", "partial", "columns", "near", "far"):
        if name not in done:
            stages[name]()

    def wait_col(off):
        rs = 2 * lax.rem(chip + off, chips) + 1 - k
        arrived(colp_ref.at[rs], col_recv.at[rs])

    def wait_plane(off):
        other = lax.rem(plane + off, 2 * nr)
        arrived(s_ref.at[other], pln_recv.at[other])

    def wait_row(i):
        from_yh, rs = lax.div(i, nr), lax.rem(i, nr)
        for sub in range(SUB):
            arrived(rowp_ref.at[from_yh, rs, sub], row_recv.at[from_yh, rs, sub])

    each(0, chips, wait_col)
    col_own.wait()
    each(0, 2 * nr, wait_row)
    each(1, 2 * nr, wait_plane)

    @pl.when(jnp.logical_not(fixed))
    def _():
        perm.wait_send()

    def wait_ring(sub):
        for way in range(2):
            for dist in range(1, reach[way] + 1):
                ring_copy(way, dist, sub).wait_send()

    each(0, SUB, wait_ring)

    def wait_block(block):
        @pl.when(column(block) != x)
        def _():
            for sub in range(SUB):
                x_copy(block, 0, sub).wait_send()

        @pl.when(column(block) == x)
        def _():
            def one(i):
                xs, to_yh = lax.div(i, 2), lax.rem(i, 2)

                @pl.when(jnp.logical_not((r == block) & (yh == to_yh)))
                def _():
                    for sub in range(SUB):
                        row_copy(block, xs, sub, piece(block, 0, sub), to_yh).wait_send()

            each(0, 2 * nx, one)

    each(0, nz, wait_block)

    def wait_chip(off):
        col_copy(off).wait_send()
        pag_copy(off).wait_send()

    def wait_near(off):
        near_copy(off).wait_send()
        nearq_copy(off).wait_send()

    def wait_far(off):
        far_copy(off).wait_send()
        farq_copy(off).wait_send()

    pair_copy.wait_send()
    each(1, chips, wait_chip)
    each(0, chips, lambda off: arrived(a_ref, col_send.at[chips + off]))
    each(1, ngroup, wait_near)
    each(1, nfar, wait_far)
    each(1, 2 * nr, lambda off: pln_copy(off).wait_send())


def exchange(activations, down_weight, keep_mask):
    nx = lax.axis_size("row_1")
    nz = lax.axis_size("col_0")
    nr = 4 * nx
    chips = 2 * nx
    rows, width = activations.shape
    own, out = down_weight.shape
    half = rows // 2
    sub_rows = rows // SUB
    reach = nz // 2
    ngroup = 4 * NEAR
    nfar = nz // NEAR
    dma = pltpu.SemaphoreType.DMA
    vmem = pl.BlockSpec(memory_space=pltpu.VMEM)
    hbm = pl.BlockSpec(memory_space=pl.ANY)
    return pl.pallas_call(
        functools.partial(exchange_kernel, nx, nz),
        out_shape=(
            jax.ShapeDtypeStruct((2, nr, SUB, sub_rows, width), BF16),
            jax.ShapeDtypeStruct((nr, rows, width), BF16),
            jax.ShapeDtypeStruct((2 * nr, half, out), BF16),
            jax.ShapeDtypeStruct((1, 128), F32),
        ),
        in_specs=[vmem] * 3,
        out_specs=(hbm, hbm, vmem, vmem),
        scratch_shapes=[
            pltpu.VMEM((nz, SUB, sub_rows, width), BF16),
            pltpu.VMEM((4, nx, SUB, sub_rows, width), BF16),
            pltpu.VMEM((rows, width), BF16),
            pltpu.VMEM((own + 8, out), BF16),
            pltpu.VMEM((nr, own + 8, out), BF16),
            pltpu.VMEM((width, out), F32),
            pltpu.VMEM((rows, out), F32),
            pltpu.VMEM((2, 2, half, out), BF16),
            pltpu.VMEM((ngroup, half, out), BF16),
            pltpu.VMEM((1, 128), F32),
            pltpu.VMEM((ngroup, 1, 128), F32),
            pltpu.VMEM((nfar, half, out), BF16),
            pltpu.VMEM((nfar, 1, 128), F32),
            dma((2, reach, SUB)),
            dma((2, reach, SUB)),
            dma((nz, SUB)),
            dma((4, nx, SUB)),
            dma((4, nx, 2, SUB)),
            dma((2, nr, SUB)),
            dma((2 * chips,)),
            dma((nr,)),
            dma((2,)),
            dma((2,)),
            dma((chips,)),
            dma((nr,)),
            dma((ngroup,)),
            dma((ngroup,)),
            dma((ngroup,)),
            dma((ngroup,)),
            dma((nfar,)),
            dma((nfar,)),
            dma((nfar,)),
            dma((nfar,)),
            dma((2 * nr,)),
            dma((2 * nr,)),
        ],
        compiler_params=pltpu.CompilerParams(collective_id=0, has_side_effects=True),
        name="exchange",
    )(activations, down_weight, keep_mask)


def products_kernel(samples, count, row_ref, col_ref, s_ref, q_ref, dw_ref, mask_ref, gram_ref, upd_ref, drop):
    part = pl.program_id(0)
    width = col_ref.shape[1]
    own = dw_ref.shape[0]
    row_count = lax.axis_size(ROW)
    r, c = lax.axis_index(ROW), lax.axis_index(COL)
    mean_square = q_ref[...] / count + 1e-06
    damping = jnp.where(2 * r + part == c, 1.0, 0.0) * (damp_ratio * mean_square)
    eye = lax.broadcasted_iota(jnp.int32, (128, 128), 0) == lax.broadcasted_iota(jnp.int32, (128, 128), 1)
    extra = jnp.where(eye, jnp.broadcast_to(damping, (128, 128)), 0.0)
    over_rows = (((0,), (0,)), ((), ()))
    for tile in range(width // 128):
        low = tile * 128
        gram = lax.dot_general(row_ref[0, :, low : low + 128], col_ref[...], over_rows, preferred_element_type=F32)
        gram = gram / samples
        gram_ref[low : low + 128, :] = gram.astype(BF16)
        gram_ref[low : low + 128, low : low + 128] = (gram[:, low : low + 128] + extra).astype(BF16)

    first = lax.rem(c, row_count) * own

    @pl.when(part == lax.div(c, row_count))
    def _():
        low = jnp.minimum(lax.div(first, 128) * 128, width - 256)
        window = row_ref[0, :, pl.ds(pl.multiple_of(low, 128), 256)]
        drop[...] = lax.dot_general(window, s_ref[...], over_rows, preferred_element_type=F32) / samples
        descent = drop[pl.ds(pl.multiple_of(first - low, 8), own), :]
        scale = jnp.broadcast_to((1.0 + damp_ratio) * mean_square[:, 0:1], descent.shape)
        updated = dw_ref[...].astype(F32) + step_ratio * descent / scale
        upd_ref[...] = (mask_ref[...].astype(F32) * updated).astype(BF16)


def products(row_panels, col_panel, s, squares, down_weight, keep_mask, count):
    _, samples, width = row_panels.shape
    own, out = down_weight.shape

    def whole(shape):
        return pl.BlockSpec(shape, lambda part: (0,) * len(shape))

    return pl.pallas_call(
        functools.partial(products_kernel, samples, count),
        out_shape=(jax.ShapeDtypeStruct((2 * width, width), BF16), jax.ShapeDtypeStruct((own, out), BF16)),
        grid=(2,),
        in_specs=[
            pl.BlockSpec((1, samples, width), lambda part: (part, 0, 0)),
            whole(col_panel.shape),
            whole(s.shape),
            whole(squares.shape),
            whole(down_weight.shape),
            whole(keep_mask.shape),
        ],
        out_specs=(pl.BlockSpec((width, width), lambda part: (part, 0)), whole((own, out))),
        scratch_shapes=[pltpu.VMEM((256, out), F32)],
        name="products",
    )(row_panels, col_panel, s, squares, down_weight, keep_mask)


def local(activations, down_weight, keep_mask):
    rows, width = activations.shape
    samples = rows * lax.axis_size(ROW)
    out = down_weight.shape[1]
    row_panels, col_panel, s, squares = exchange(activations, down_weight, keep_mask)
    return products(
        row_panels.reshape(2, samples, width),
        col_panel.reshape(samples, width),
        s.reshape(samples, out),
        squares,
        down_weight,
        keep_mask,
        samples * width * lax.axis_size(COL),
    )


def solution(mesh):
    torus = Mesh(mesh.devices.reshape(2, 4, 2, 16, 2), AXES)
    in_specs = (P(ROW, COL), P(AXES, None), P(AXES, None))
    out_specs = (P(ROW, COL), P(AXES, None))
    return jax.shard_map(local, mesh=torus, in_specs=in_specs, out_specs=out_specs, check_vma=False)
```

time: 92.9 us -> 79.5 us (0.86)
  the two profiles are of different devices: /device:TPU:24 before, /device:TPU:25 now
where the time goes in v2:
time: 79.5 us; the launch traced here: 79.3 us
  Pallas kernels  78.7 us (99%)
    pallas_call x1, Pallas kernels, exchange(): pl.pallas_call(functools.partial(exchange_kernel, nx, nz), out_shape=(jax...  73.3 us
    pallas_call x1, Pallas kernels, products(): pl.pallas_call(functools.partial(products_kernel, samples, count), out_sh...  5.4 us

profile of v2, /device:TPU:25, one launch (start us, length us, event | category | flops | bytes accessed | tf_op | source)
XLA Modules:
  0.0 79.3 jit_solution(8747916468783501645)
XLA Ops:
  0.6 73.3 %exchange.1 = (bf16[2,16,2,16,896]{4,3,2,1,0:T(8,128)(2,1)}, bf16[16,32,896]{2,1,0:T(8,128)(2,1)}, bf16[32,16,256]{2,1,0:T(8,128)(2,1)}, f32[1,128]{1,0:T(1,128)}) custom-call(bf16[32,896]{1,0:T(8,128)(2,1)} %a_ref.1, bf16[56,256]{1,0:T(8,128)(2,1)} %dw_ref.3, s32[56,256]{1,0:T(8,128)} %mask_ref.3), custom_call_target="tpu_custom_call" | custom-call | tf_op jit(solution)/shard_map/exchange/pallas_call | solution.py:492
  73.9 5.4 %products.1 = (bf16[1792,896]{1,0:T(8,128)(2,1)}, bf16[56,256]{1,0:T(8,128)(2,1)}) custom-call(bf16[2,512,896]{2,1,0:T(8,128)(2,1)} %bitcast.3, bf16[512,896]{1,0:T(8,128)(2,1)} %bitcast.4, bf16[512,256]{1,0:T(8,128)(2,1)} %bitcast.5, f32[1,128]{1,0:T(1,128)} %get-tuple-element.9.q_ref, bf16[56,256]{1,0:T(8,128)(2,1)} %dw_ref.3, s32[56,256]{1,0:T(8,128)} %mask_ref.3), custom_call_target="tpu_custom_call" | custom-call | tf_op jit(solution)/shard_map/products/pallas_call | solution.py:582

commit v3 on v2

--- a/solution.py
+++ b/solution.py
@@ -14,9 +14,10 @@
 COL = AXES[3:]
 F32 = jnp.float32
 BF16 = jnp.bfloat16
-SUB = 2
+SUB = 1
 NEAR = 4
-AFTER = {1: ("weights",), 2: ("partial",), 3: ("columns", "near")}
+AFTER = {1: ("weights",), 2: ("partial",)}
+LATER = {3: ("near", "columns")}
 
 damp_ratio = 0.1
 step_ratio = 0.25
@@ -289,9 +290,17 @@
                         arrived(zbuf.at[block, sub], ring_recv.at[way, dist - 1, sub])
                         if dist == far:
                             ring_from(way, dist, sub)
-                        spread(block, dist, sub)
 
             each(0, SUB, one)
+
+    def spread_round(t):
+        def one(sub):
+            for dist in (2 * t + 2, 2 * t + 1):
+                for way in range(2):
+                    if dist <= reach[way]:
+                        spread(block_at(way, dist), dist, sub)
+
+        each(0, SUB, one)
 
     def relay_round(t):
         for dist in (2 * t, 2 * t - 1) if t else (0,):
@@ -396,8 +405,12 @@
     rounds = (reach[0] + 1) // 2
     for t in range(rounds):
         ring_round(t)
+        for name in AFTER.get(t, ()):
+            stages[name]()
+            done.append(name)
+        spread_round(t)
         relay_round(t)
-        for name in AFTER.get(t, ()):
+        for name in LATER.get(t, ()):
             stages[name]()
             done.append(name)
     relay_round(rounds)
@@ -555,7 +568,7 @@
     for tile in range(width // 128):
         low = tile * 128
         gram = lax.dot_general(row_ref[0, :, low : low + 128], col_ref[...], over_rows, preferred_element_type=F32)
-        gram = gram / samples
+        gram = gram * (1.0 / samples)
         gram_ref[low : low + 128, :] = gram.astype(BF16)
         gram_ref[low : low + 128, low : low + 128] = (gram[:, low : low + 128] + extra).astype(BF16)
 
@@ -565,7 +578,7 @@
     def _():
         low = jnp.minimum(lax.div(first, 128) * 128, width - 256)
         window = row_ref[0, :, pl.ds(pl.multiple_of(low, 128), 256)]
-        drop[...] = lax.dot_general(window, s_ref[...], over_rows, preferred_element_type=F32) / samples
+        drop[...] = lax.dot_general(window, s_ref[...], over_rows, preferred_element_type=F32) * (1.0 / samples)
         descent = drop[pl.ds(pl.multiple_of(first - low, 8), own), :]
         scale = jnp.broadcast_to((1.0 + damp_ratio) * mean_square[:, 0:1], descent.shape)
         updated = dw_ref[...].astype(F32) + step_ratio * descent / scale

time: 79.5 us -> 76.6 us (0.964)
  the two profiles are of different devices: /device:TPU:25 before, /device:TPU:7 now
where the time goes in v3:
time: 76.6 us; the launch traced here: 76.4 us
  Pallas kernels  75.7 us (99%)
    pallas_call x1, Pallas kernels, exchange(): pl.pallas_call(functools.partial(exchange_kernel, nx, nz), out_shape=(jax...  70.3 us
    pallas_call x1, Pallas kernels, products(): pl.pallas_call(functools.partial(products_kernel, samples, count), out_sh...  5.4 us

profile of v3, /device:TPU:7, one launch (start us, length us, event | category | flops | bytes accessed | tf_op | source)
XLA Modules:
  0.0 76.4 jit_solution(10874251066892724630)
XLA Ops:
  0.6 70.3 %exchange.1 = (bf16[2,16,1,32,896]{4,3,2,1,0:T(8,128)(2,1)}, bf16[16,32,896]{2,1,0:T(8,128)(2,1)}, bf16[32,16,256]{2,1,0:T(8,128)(2,1)}, f32[1,128]{1,0:T(1,128)}) custom-call(bf16[32,896]{1,0:T(8,128)(2,1)} %a_ref.1, bf16[56,256]{1,0:T(8,128)(2,1)} %dw_ref.3, s32[56,256]{1,0:T(8,128)} %mask_ref.3), custom_call_target="tpu_custom_call" | custom-call | tf_op jit(solution)/shard_map/exchange/pallas_call | solution.py:505
  71.0 5.4 %products.1 = (bf16[1792,896]{1,0:T(8,128)(2,1)}, bf16[56,256]{1,0:T(8,128)(2,1)}) custom-call(bf16[2,512,896]{2,1,0:T(8,128)(2,1)} %bitcast.3, bf16[512,896]{1,0:T(8,128)(2,1)} %bitcast.4, bf16[512,256]{1,0:T(8,128)(2,1)} %bitcast.5, f32[1,128]{1,0:T(1,128)} %get-tuple-element.9.q_ref, bf16[56,256]{1,0:T(8,128)(2,1)} %dw_ref.3, s32[56,256]{1,0:T(8,128)} %mask_ref.3), custom_call_target="tpu_custom_call" | custom-call | tf_op jit(solution)/shard_map/products/pallas_call | solution.py:595

commit v4 on v3

--- a/solution.py
+++ b/solution.py
@@ -210,7 +210,8 @@
         )
 
     def deliver(block, xs, sub, src):
-        def one(to_yh):
+        def one(turn):
+            to_yh = lax.rem(turn + k, 2)
             here = (block == r) & (yh == to_yh)
 
             @pl.when(jnp.logical_not(here))

time: 76.6 us -> 76.6 us (level)
  no operation moved by 1% of the time
where the time goes in v4:
time: 76.6 us; the launch traced here: 76.4 us
  Pallas kernels  75.7 us (99%)
    pallas_call x1, Pallas kernels, exchange(): pl.pallas_call(functools.partial(exchange_kernel, nx, nz), out_shape=(jax...  70.3 us
    pallas_call x1, Pallas kernels, products(): pl.pallas_call(functools.partial(products_kernel, samples, count), out_sh...  5.4 us

profile of v4, /device:TPU:7, one launch (start us, length us, event | category | flops | bytes accessed | tf_op | source)
XLA Modules:
  0.0 76.4 jit_solution(1803608779649013680)
XLA Ops:
  0.6 70.3 %exchange.1 = (bf16[2,16,1,32,896]{4,3,2,1,0:T(8,128)(2,1)}, bf16[16,32,896]{2,1,0:T(8,128)(2,1)}, bf16[32,16,256]{2,1,0:T(8,128)(2,1)}, f32[1,128]{1,0:T(1,128)}) custom-call(bf16[32,896]{1,0:T(8,128)(2,1)} %a_ref.1, bf16[56,256]{1,0:T(8,128)(2,1)} %dw_ref.3, s32[56,256]{1,0:T(8,128)} %mask_ref.3), custom_call_target="tpu_custom_call" | custom-call | tf_op jit(solution)/shard_map/exchange/pallas_call | solution.py:506
  71.0 5.4 %products.1 = (bf16[1792,896]{1,0:T(8,128)(2,1)}, bf16[56,256]{1,0:T(8,128)(2,1)}) custom-call(bf16[2,512,896]{2,1,0:T(8,128)(2,1)} %bitcast.3, bf16[512,896]{1,0:T(8,128)(2,1)} %bitcast.4, bf16[512,256]{1,0:T(8,128)(2,1)} %bitcast.5, f32[1,128]{1,0:T(1,128)} %get-tuple-element.9.q_ref, bf16[56,256]{1,0:T(8,128)(2,1)} %dw_ref.3, s32[56,256]{1,0:T(8,128)} %mask_ref.3), custom_call_target="tpu_custom_call" | custom-call | tf_op jit(solution)/shard_map/products/pallas_call | solution.py:596
